TPU v7x, 32 devices: a whole 2x2x4 slice. The times are simulated.
32 devices in a mesh: groups: 2 (over y), blk: 4 (over z), tile: 2 (over x), pair: 2 (over core).
Axes of the slice: x: 2, y: 2, z: 4, core: 2. Of those that a mesh axis runs over, the one named last changes fastest.
Arguments:
- left_tokens: bfloat16 [4, 1536, 768], P(('groups', 'pair'), 'blk', 'tile'), parts along dimension 0, may hold values from -32 to 32
- right_tokens: bfloat16 [4, 1536, 768], P(('groups', 'pair'), 'blk', 'tile'), parts along dimension 0, may hold values from -32 to 32
- self_qkv: bfloat16 [3, 768, 512], P(None, None, 'tile'), may hold values from -1 to 1
- self_out: bfloat16 [512, 768], P('tile'), may hold values from -0.25 to 0.25
- cross_qkv: bfloat16 [3, 768, 512], P(None, None, 'tile'), may hold values from -1 to 1
- cross_out: bfloat16 [512, 768], P('tile'), may hold values from -0.25 to 0.25
- reassemble: bfloat16 [768, 256], P('tile'), may hold values from -0.21875 to 0.21875
- conv_weight: bfloat16 [3, 3, 256, 256], replicated, may hold values from -0.125 to 0.125
Outputs:
- joined: bfloat16 [4, 12, 128, 256], P(('groups', 'pair'), 'blk', 'tile'), parts along dimension 0
There are 2 independent parts, one for each index of `groups`. A program takes and returns all parts, laid end to end along the dimension named above; an argument that names none is the same for every part. Nothing has to cross between parts.
All inputs are finite; a program needn't handle non-finite values.
Results may differ from a plain program's by a relative error of at most 0.018.
Values may be sent and summed in bfloat16 or wider, within the bound.
A program may use at most 64 MiB of HBM per device.

v0:
```python
import jax
import jax.numpy as jnp
from jax import lax
from jax.sharding import PartitionSpec as P

HD = 64
CH = 256
GRID_W = 128


def padded_2(cells, sides, width):
    for axis, dim in sides:
        count = lax.axis_size(axis)
        ends = count - 1
        head = lax.slice_in_dim(cells, 0, width, axis=dim)
        tail = lax.slice_in_dim(cells, cells.shape[dim] - width, cells.shape[dim], axis=dim)
        cells = jnp.concatenate(
            [
                lax.ppermute(tail, axis, [(i, (i + 1) % count) for i in range(ends)]),
                cells,
                lax.ppermute(head, axis, [((i + 1) % count, i) for i in range(ends)]),
            ],
            axis=dim,
        )
    return cells


def layer_norm(values):
    widened = values.astype(jnp.float32)
    centred = widened - jnp.mean(widened, axis=-1, keepdims=True)
    variance = jnp.mean(centred * centred, axis=-1, keepdims=True)
    return (centred * lax.rsqrt(variance + 1e-06)).astype(jnp.bfloat16)


def project_rows(normed, weight):
    return jnp.dot(normed, weight, preferred_element_type=jnp.float32).astype(jnp.bfloat16)


def initial_state(queries):
    query_count = queries.shape[0]
    head_count = queries.shape[1] // HD
    return (
        jnp.full((head_count, query_count), -1e30, jnp.float32),
        jnp.zeros((head_count, query_count), jnp.float32),
        jnp.zeros(queries.shape, jnp.float32),
    )


def attend_keys(running, queries, keys_rows, values_rows):
    maxima, totals, accumulated = running
    query_count = queries.shape[0]
    head_count = queries.shape[1] // HD
    key_count = keys_rows.shape[0]
    scores = jnp.einsum(
        "qhd,khd->hqk",
        queries.reshape(query_count, head_count, HD),
        keys_rows.reshape(key_count, head_count, HD),
        preferred_element_type=jnp.float32,
    ) * HD ** (-0.5)
    new_maxima = jnp.maximum(maxima, jnp.max(scores, axis=2))
    correction = jnp.exp(maxima - new_maxima)
    expanded = jnp.exp(scores - new_maxima[:, :, None])
    totals = totals * correction + jnp.sum(expanded, axis=2)
    mixed = jnp.einsum(
        "hqk,khd->qhd",
        expanded.astype(jnp.bfloat16),
        values_rows.reshape(key_count, head_count, HD),
        preferred_element_type=jnp.float32,
    )
    accumulated = (
        accumulated.reshape(query_count, head_count, HD) * correction.T[:, :, None] + mixed
    )
    return (new_maxima, totals, accumulated.reshape(query_count, head_count * HD))


def fold_keys(running, queries, keys_rows, values_rows):
    key_count = keys_rows.shape[0]
    block_rows = max((divisor for divisor in range(1, 1025) if key_count % divisor == 0))
    if block_rows == key_count:
        return attend_keys(running, queries, keys_rows, values_rows)
    stacked_keys = keys_rows.reshape(key_count // block_rows, block_rows, keys_rows.shape[1])
    stacked_values = values_rows.reshape(key_count // block_rows, block_rows, values_rows.shape[1])

    def step_block(current, blocks):
        return (attend_keys(current, queries, blocks[0], blocks[1]), None)

    result, unused = lax.scan(step_block, running, (stacked_keys, stacked_values))
    return result


def finish_state(running):
    maxima, totals, accumulated = running
    query_count = accumulated.shape[0]
    head_count = accumulated.shape[1] // HD
    normalized = accumulated.reshape(query_count, head_count, HD) / totals.T[:, :, None]
    return normalized.reshape(query_count, head_count * HD).astype(jnp.bfloat16)


def body(
    left_tokens, right_tokens, self_qkv, self_out, cross_qkv, cross_out, reassemble, conv_weight
):
    left_full, right_full = (
        lax.all_gather(left_tokens, "tile", axis=2, tiled=True),
        lax.all_gather(right_tokens, "tile", axis=2, tiled=True),
    )
    left_rows = left_full[0]
    left_normed = layer_norm(left_rows)
    right_normed = layer_norm(right_full[0])
    self_query = project_rows(left_normed, self_qkv[0])
    self_key = project_rows(left_normed, self_qkv[1])
    self_value = project_rows(left_normed, self_qkv[2])
    cross_key = project_rows(right_normed, cross_qkv[1])
    cross_value = project_rows(right_normed, cross_qkv[2])
    pieces = (
        lax.all_gather(self_key, "blk", axis=0, tiled=True),
        lax.all_gather(self_value, "blk", axis=0, tiled=True),
    )
    self_state = fold_keys(initial_state(self_query), self_query, pieces[0], pieces[1])
    self_mixed = finish_state(self_state)
    self_term = jnp.dot(self_mixed, self_out, preferred_element_type=jnp.float32)
    self_share = lax.psum_scatter(
        self_term.astype(jnp.bfloat16), "tile", scatter_dimension=1, tiled=True
    ).astype(jnp.float32)
    updated = (left_tokens[0].astype(jnp.float32) + self_share).astype(jnp.bfloat16)
    updated_full = lax.all_gather(updated, "tile", axis=1, tiled=True)
    updated_normed = layer_norm(updated_full)
    cross_query = project_rows(updated_normed, cross_qkv[0])
    pieces = (
        lax.all_gather(cross_key, "blk", axis=0, tiled=True),
        lax.all_gather(cross_value, "blk", axis=0, tiled=True),
    )
    cross_state = fold_keys(initial_state(cross_query), cross_query, pieces[0], pieces[1])
    cross_mixed = finish_state(cross_state)
    cross_share = lax.psum_scatter(
        jnp.dot(cross_mixed, cross_out, preferred_element_type=jnp.float32).astype(jnp.bfloat16),
        "tile",
        scatter_dimension=1,
        tiled=True,
    ).astype(jnp.float32)
    final_tokens = (updated.astype(jnp.float32) + cross_share).astype(jnp.bfloat16)
    band_rows = final_tokens.shape[0] // GRID_W
    partial_map = jnp.dot(final_tokens, reassemble, preferred_element_type=jnp.float32).reshape(
        band_rows, GRID_W, CH
    )
    feature_map = lax.psum_scatter(
        partial_map.astype(jnp.bfloat16), "tile", scatter_dimension=1, tiled=True
    )
    column_count = feature_map.shape[1]
    activated = jnp.maximum(feature_map, jnp.zeros((), jnp.bfloat16))
    padded = padded_2(activated, (("blk", 0), ("tile", 1)), 1)
    stacked = jnp.concatenate(
        [
            padded[row_shift : row_shift + band_rows, col_shift : col_shift + column_count]
            for row_shift in range(3)
            for col_shift in range(3)
        ],
        axis=-1,
    )
    convolved = jnp.dot(
        stacked.reshape(band_rows * column_count, 9 * CH),
        conv_weight.reshape(9 * CH, CH),
        preferred_element_type=jnp.float32,
    )
    joined = (
        feature_map.astype(jnp.float32) + convolved.reshape(band_rows, column_count, CH)
    ).astype(jnp.bfloat16)
    return joined[None]


def solution(mesh):
    placed = (
        P(("groups", "pair"), "blk", "tile"),
        P(("groups", "pair"), "blk", "tile"),
        P(None, None, "tile"),
        P("tile", None),
        P(None, None, "tile"),
        P("tile", None),
        P("tile", None),
        P(),
    )
    return jax.shard_map(
        body,
        mesh=mesh,
        in_specs=placed,
        out_specs=P(("groups", "pair"), "blk", "tile", None),
        check_vma=False,
    )
```

profile of v0, /device:TPU:0, one launch (start us, length us, event | category | flops | bytes accessed | tf_op | source)
XLA Modules:
  0.0 217.8 jit_solution(9744858873867985740)
XLA Ops:
  6.5 11.0 %all_gather.21 = bf16[1,384,768]{2,1,0:T(8,128)(2,1)S(1)} all-gather(bf16[1,384,384]{2,1,0:T(8,128)(2,1)} %param.12), channel_id=1, replica_groups=mesh['groups'=2,'blk'=4,'tile'=2,'pair'=2] {'tile'}, dimensions={2}, use_global_device_ids=true | all-gather | bytes 884736 | tf_op jit(solution)/shard_map/all_gather | solution.py:103
  18.1 1.4 convolution_convert_fusion.8
  20.3 20.0 %all_gather.22 = bf16[1536,256]{1,0:T(8,128)(2,1)S(1)} all-gather(bf16[384,256]{1,0:T(8,128)(2,1)S(1)} %convolution_convert_fusion.8), channel_id=1, replica_groups=mesh['groups'=2,'blk'=4,'tile'=2,'pair'=2] {'blk'}, dimensions={0}, use_global_device_ids=true | all-gather | bytes 983040 | tf_op jit(solution)/shard_map/all_gather | solution.py:115
  40.3 18.1 %all_gather.23 = bf16[1536,256]{1,0:T(8,128)(2,1)} all-gather(bf16[384,256]{1,0:T(8,128)(2,1)S(1)} %convolution_convert_fusion.6), channel_id=1, replica_groups=mesh['groups'=2,'blk'=4,'tile'=2,'pair'=2] {'blk'}, dimensions={0}, use_global_device_ids=true | all-gather | bytes 983040 | tf_op jit(solution)/shard_map/all_gather | solution.py:116
  58.4 0.8 copy.20
  59.3 19.8 %while.30 = (s32[]{:T(128)}, f32[4,384]{1,0:T(4,128)S(1)}, f32[4,384]{1,0:T(4,128)S(1)}, f32[384,256]{0,1:T(8,128)S(1)}, bf16[2,768,256]{2,1,0:T(8,128)(2,1)S(1)...) while((s32[]{:T(128)}, f32[4,384]{1,0:T(4,128)S(1)}, ...), condition=%wide.region_5.0_spmd.clone, body=%wide.region_2.5_spmd.clone.sunk | while | flops 311632896 | bytes 38043784 | solution.py:87
  59.3 1.1 constant_dynamic-slice_fusion.6
  60.5 3.9 %bitcast_reduce_fusion.4 = (f32[4,384]{1,0:T(4,128)S(1)}, f32[4,768,384]{2,1,0:T(8,128)}) fusion(bf16[768,4,64]{0,2,1:T(8,128)(2,1)S(1)} %bitcast.186, bf16[384,4,64]{0,2,1:T(8,128)(2,1)} %bitcast.199), kind=kOutput, calls=%fused_computation.1.clone.1 | convolution fusion | flops 153352704 | bytes 5314560 | tf_op jit(solution)/shard_map/while/body/eval_jaxpr/qhd,khd->hqk/dot_general | solution.py:54
  64.6 3.5 %fusion.112 = f32[384,4,64]{0,2,1:T(8,128)S(1)} fusion(bf16[768,4,64]{0,2,1:T(8,128)(2,1)S(1)} %bitcast.187, f32[4,768,384]{2,1,0:T(8,128)} %get-tuple-element.301, f32[4,384]{1,0:T(4,128)S(1)} %get-tuple-element.336, f32[384,4,64]{0,2,1:T(8,128)S(1)} %bitcast.192, f32[384,4]{0,1:T(4,128)S(1)} %get-tuple-element.303), kind=kOutput, calls=%fused_computation.9.clone.1 | convolution fusion | flops 154730496 | bytes 5910528 | tf_op jit(solution)/shard_map/while/body/eval_jaxpr/hqk,khd->qhd/dot_general | solution.py:64
  68.3 0.8 fusion.110
  69.2 1.1 constant_dynamic-slice_fusion.6
  70.4 3.9 %bitcast_reduce_fusion.4 = (f32[4,384]{1,0:T(4,128)S(1)}, f32[4,768,384]{2,1,0:T(8,128)}) fusion(bf16[768,4,64]{0,2,1:T(8,128)(2,1)S(1)} %bitcast.186, bf16[384,4,64]{0,2,1:T(8,128)(2,1)} %bitcast.199), kind=kOutput, calls=%fused_computation.1.clone.1 | convolution fusion | flops 153352704 | bytes 5314560 | tf_op jit(solution)/shard_map/while/body/eval_jaxpr/qhd,khd->hqk/dot_general | solution.py:54
  74.5 3.5 %fusion.112 = f32[384,4,64]{0,2,1:T(8,128)S(1)} fusion(bf16[768,4,64]{0,2,1:T(8,128)(2,1)S(1)} %bitcast.187, f32[4,768,384]{2,1,0:T(8,128)} %get-tuple-element.301, f32[4,384]{1,0:T(4,128)S(1)} %get-tuple-element.336, f32[384,4,64]{0,2,1:T(8,128)S(1)} %bitcast.192, f32[384,4]{0,1:T(4,128)S(1)} %get-tuple-element.303), kind=kOutput, calls=%fused_computation.9.clone.1 | convolution fusion | flops 154730496 | bytes 5910528 | tf_op jit(solution)/shard_map/while/body/eval_jaxpr/hqk,khd->qhd/dot_general | solution.py:64
  78.2 0.8 fusion.110
  79.1 1.4 convolution_convert_fusion.1
  80.5 1.0 copy.27
  81.6 9.7 %all_gather.24 = bf16[1,384,768]{2,1,0:T(8,128)(2,1)S(1)} all-gather(bf16[1,384,384]{2,1,0:T(8,128)(2,1)S(1)} %copy-done.7), channel_id=1, replica_groups=mesh['groups'=2,'blk'=4,'tile'=2,'pair'=2] {'tile'}, dimensions={2}, use_global_device_ids=true | all-gather | bytes 884736 | tf_op jit(solution)/shard_map/all_gather | solution.py:104
  91.8 1.4 convolution_convert_fusion.3
  93.2 1.4 convolution_convert_fusion.5
  94.6 17.3 %all_gather.27 = bf16[1536,256]{1,0:T(8,128)(2,1)S(1)} all-gather(bf16[384,256]{1,0:T(8,128)(2,1)S(1)} %convolution_convert_fusion.3), channel_id=1, replica_groups=mesh['groups'=2,'blk'=4,'tile'=2,'pair'=2] {'blk'}, dimensions={0}, use_global_device_ids=true | all-gather | bytes 983040 | tf_op jit(solution)/shard_map/all_gather | solution.py:130
  111.9 16.3 %all_gather.25 = bf16[1536,256]{1,0:T(8,128)(2,1)} all-gather(bf16[384,256]{1,0:T(8,128)(2,1)S(1)} %convolution_convert_fusion.5), channel_id=1, replica_groups=mesh['groups'=2,'blk'=4,'tile'=2,'pair'=2] {'blk'}, dimensions={0}, use_global_device_ids=true | all-gather | bytes 983040 | tf_op jit(solution)/shard_map/all_gather | solution.py:129
  128.2 1.2 copy.28
  130.2 8.4 %all_gather.26 = bf16[384,768]{1,0:T(8,128)(2,1)S(1)} all-gather(bf16[384,384]{1,0:T(8,128)(2,1)S(1)} %fusion.51), channel_id=1, replica_groups=mesh['groups'=2,'blk'=4,'tile'=2,'pair'=2] {'tile'}, dimensions={1}, use_global_device_ids=true | all-gather | bytes 884736 | tf_op jit(solution)/shard_map/all_gather | solution.py:125
  139.1 1.4 convolution_convert_fusion.4
  140.4 0.8 copy.23
  141.3 19.8 %while.31 = (s32[]{:T(128)}, f32[4,384]{1,0:T(4,128)S(1)}, f32[4,384]{1,0:T(4,128)S(1)}, f32[384,256]{0,1:T(8,128)S(1)}, bf16[2,768,256]{2,1,0:T(8,128)(2,1)}, /...) while((s32[]{:T(128)}, f32[4,384]{1,0:T(4,128)S(1)}, ...), condition=%wide.region_14.15_spmd.clone, body=%wide.region_11.14_spmd.clone.sunk | while | flops 311632896 | bytes 38043784 | solution.py:87
  141.3 1.1 constant_dynamic-slice_fusion.7
  142.6 3.9 %bitcast_reduce_fusion.5 = (f32[4,384]{1,0:T(4,128)S(1)}, f32[4,768,384]{2,1,0:T(8,128)}) fusion(bf16[768,4,64]{0,2,1:T(8,128)(2,1)S(1)} %bitcast.188, bf16[384,4,64]{0,2,1:T(8,128)(2,1)} %bitcast.198), kind=kOutput, calls=%fused_computation.19.clone.1 | convolution fusion | flops 153352704 | bytes 5314560 | tf_op jit(solution)/shard_map/while/body/eval_jaxpr/qhd,khd->hqk/dot_general | solution.py:54
  146.6 3.5 %fusion.120 = f32[384,4,64]{0,2,1:T(8,128)S(1)} fusion(bf16[768,4,64]{0,2,1:T(8,128)(2,1)S(1)} %bitcast.189, f32[4,768,384]{2,1,0:T(8,128)} %get-tuple-element.314, f32[4,384]{1,0:T(4,128)S(1)} %get-tuple-element.363, f32[384,4,64]{0,2,1:T(8,128)S(1)} %bitcast.190, f32[384,4]{0,1:T(4,128)S(1)} %get-tuple-element.316), kind=kOutput, calls=%fused_computation.27.clone.1 | convolution fusion | flops 154730496 | bytes 5910528 | tf_op jit(solution)/shard_map/while/body/eval_jaxpr/hqk,khd->qhd/dot_general | solution.py:64
  150.4 0.8 fusion.118
  151.2 1.1 constant_dynamic-slice_fusion.7
  152.4 3.9 %bitcast_reduce_fusion.5 = (f32[4,384]{1,0:T(4,128)S(1)}, f32[4,768,384]{2,1,0:T(8,128)}) fusion(bf16[768,4,64]{0,2,1:T(8,128)(2,1)S(1)} %bitcast.188, bf16[384,4,64]{0,2,1:T(8,128)(2,1)} %bitcast.198), kind=kOutput, calls=%fused_computation.19.clone.1 | convolution fusion | flops 153352704 | bytes 5314560 | tf_op jit(solution)/shard_map/while/body/eval_jaxpr/qhd,khd->hqk/dot_general | solution.py:54
  156.5 3.5 %fusion.120 = f32[384,4,64]{0,2,1:T(8,128)S(1)} fusion(bf16[768,4,64]{0,2,1:T(8,128)(2,1)S(1)} %bitcast.189, f32[4,768,384]{2,1,0:T(8,128)} %get-tuple-element.314, f32[4,384]{1,0:T(4,128)S(1)} %get-tuple-element.363, f32[384,4,64]{0,2,1:T(8,128)S(1)} %bitcast.190, f32[384,4]{0,1:T(4,128)S(1)} %get-tuple-element.316), kind=kOutput, calls=%fused_computation.27.clone.1 | convolution fusion | flops 154730496 | bytes 5910528 | tf_op jit(solution)/shard_map/while/body/eval_jaxpr/hqk,khd->qhd/dot_general | solution.py:64
  160.3 0.8 fusion.118
  161.1 1.4 convolution_convert_fusion
  162.5 1.0 copy.29
  163.7 14.7 %reduce-scatter.12.cloned.1.call-done = bf16[384,384]{1,0:T(8,128)(2,1)} async-done(((bf16[768,384]{1,0:T(8,128)(2,1)}), bf16[384,384]{1,0:T(8,128)(2,1)}) %reduce-scatter.12.cloned.1.call-update) | async-done | bytes 294928
  178.4 1.2 copy.30
  179.6 0.9 convolution_convert_fusion.2
  180.5 11.2 %reduce-scatter.8.cloned.1.call-done = bf16[3,64,256]{2,1,0:T(8,128)(2,1)} async-done(((bf16[3,128,256]{2,1,0:T(8,128)(2,1)}), bf16[3,64,256]{2,1,0:T(8,128)(2,1)}) %reduce-scatter.8.cloned.1.call-update) | async-done | bytes 98320 | tf_op jit(solution)/shard_map/reduce_scatter | solution.py:145
  191.7 1.0 broadcast_maximum_fusion
  192.7 3.4 %collective-permute-start = (bf16[1,64,256]{2,1,0:T(8,128)(2,1)S(1)}, bf16[1,64,256]{2,1,0:T(8,128)(2,1)S(1)}, u32[]{:S(2)}, u32[]{:S(2)}) collective-permute-start(bf16[1,64,256]{2,1,0:T(8,128)(2,1)S(1)} %get-tuple-element.205), channel_id=1, source_target_pairs={{0,4},{4,8},{8,12},{1,5},{5,9},{9,13},{2,6},{6,10},{10,14},{3,7},{... | collective-permute-start | bytes 98312 | tf_op jit(solution)/shard_map/ppermute | solution.py:19
  196.1 1.3 collective-permute-start.1
  197.7 4.2 %collective-permute-done.1 = bf16[1,64,256]{2,1,0:T(8,128)(2,1)S(1)} collective-permute-done((bf16[1,64,256]{2,1,0:T(8,128)(2,1)S(1)}, bf16[1,64,256]{2,1,0:T(8,128)(2,1)S(1)}, u32[]{:S(2)}, u32[]{:S(2)}) %collective-permute-start.1) | collective-permute-done | bytes 32800 | tf_op jit(solution)/shard_map/ppermute | solution.py:21
  201.9 2.5 %collective-permute-start.2 = (bf16[5,1,256]{2,1,0:T(2,128)(2,1)S(1)}, bf16[5,1,256]{2,1,0:T(2,128)(2,1)S(1)}, u32[]{:S(2)}, u32[]{:S(2)}) collective-permute-start(bf16[5,1,256]{2,1,0:T(2,128)(2,1)S(1)} %get-tuple-element.204), channel_id=1, source_target_pairs={{0,2},{1,3},{4,6},{5,7},{8,10},{9,11},{12,14},{13,15},{16,18},{17,... | collective-permute-start | bytes 7688 | tf_op jit(solution)/shard_map/ppermute | solution.py:19
  204.4 1.3 collective-permute-start.3
  205.7 4.2 %collective-permute-done.3 = bf16[5,1,256]{2,1,0:T(2,128)(2,1)S(1)} collective-permute-done((bf16[5,1,256]{2,1,0:T(2,128)(2,1)S(1)}, bf16[5,1,256]{2,1,0:T(2,128)(2,1)S(1)}, u32[]{:S(2)}, u32[]{:S(2)}) %collective-permute-start.3) | collective-permute-done | bytes 2592 | tf_op jit(solution)/shard_map/ppermute | solution.py:21
  210.2 1.1 fusion.47
  (88 shorter events, 6.3 us)
Async XLA Ops:
  6.5 203.7 %copy-start = (bf16[3,3,256,256]{3,2,1,0:T(8,128)(2,1)S(1)}, bf16[3,3,256,256]{3,2,1,0:T(8,128)(2,1)}, u32[]{:S(2)}) copy-start(bf16[3,3,256,256]{3,2,1,0:T(8,128)(2,1)} %param.19) | copy-start | bytes 3538948
  6.5 121.6 %reduce-scatter.10.cloned.1.call-start = ((), (), s32[]{:S(2)}) async-start(), calls=%async_computation.4 | async-start | bytes 884736
  17.7 1.8 copy-start.9
  64.6 3.8 %copy-start.1 = (f32[4,768,384]{2,1,0:T(8,128)S(1)}, f32[4,768,384]{2,1,0:T(8,128)}, u32[]{:S(2)}) copy-start(f32[4,768,384]{2,1,0:T(8,128)} %get-tuple-element.301) | copy-start | bytes 14155780 | tf_op jit(solution)/shard_map/while
  74.5 3.8 %copy-start.1 = (f32[4,768,384]{2,1,0:T(8,128)S(1)}, f32[4,768,384]{2,1,0:T(8,128)}, u32[]{:S(2)}) copy-start(f32[4,768,384]{2,1,0:T(8,128)} %get-tuple-element.301) | copy-start | bytes 14155780 | tf_op jit(solution)/shard_map/while
  80.5 1.1 copy-start.7
  81.6 96.8 %reduce-scatter.12.cloned.1.call-start = ((), (), s32[]{:S(2)}) async-start(), calls=%async_computation.5 | async-start | bytes 884736
  94.6 34.8 %copy-start.5 = (bf16[1,384,384]{2,1,0:T(8,128)(2,1)S(1)}, bf16[1,384,384]{2,1,0:T(8,128)(2,1)}, u32[]{:S(2)}) copy-start(bf16[1,384,384]{2,1,0:T(8,128)(2,1)} %param.12) | copy-start | bytes 884740
  129.5 0.7 copy-start.3
  146.6 3.8 %copy-start.2 = (f32[4,768,384]{2,1,0:T(8,128)S(1)}, f32[4,768,384]{2,1,0:T(8,128)}, u32[]{:S(2)}) copy-start(f32[4,768,384]{2,1,0:T(8,128)} %get-tuple-element.314) | copy-start | bytes 14155780 | tf_op jit(solution)/shard_map/while
  156.5 3.8 %copy-start.2 = (f32[4,768,384]{2,1,0:T(8,128)S(1)}, f32[4,768,384]{2,1,0:T(8,128)}, u32[]{:S(2)}) copy-start(f32[4,768,384]{2,1,0:T(8,128)} %get-tuple-element.314) | copy-start | bytes 14155780 | tf_op jit(solution)/shard_map/while
  162.5 17.0 %copy-start.4 = (bf16[384,384]{1,0:T(8,128)(2,1)S(1)}, bf16[384,384]{1,0:T(8,128)(2,1)}, u32[]{:S(2)}) copy-start(bf16[384,384]{1,0:T(8,128)(2,1)} %copy-done.3) | copy-start | bytes 884740
  162.5 17.0 %copy-start.8 = (bf16[384,256]{1,0:T(8,128)(2,1)S(1)}, bf16[384,256]{1,0:T(8,128)(2,1)}, u32[]{:S(2)}) copy-start(bf16[384,256]{1,0:T(8,128)(2,1)} %param.18) | copy-start | bytes 589828
  163.6 28.1 %reduce-scatter.8.cloned.1.call-start = ((), (), s32[]{:S(2)}) async-start(), calls=%async_computation.3 | async-start | bytes 294912 | tf_op jit(solution)/shard_map/reduce_scatter | solution.py:145
  191.7 18.3 %copy-start.6 = (bf16[3,64,256]{2,1,0:T(8,128)(2,1)S(1)}, bf16[3,64,256]{2,1,0:T(8,128)(2,1)}, u32[]{:S(2)}) copy-start(bf16[3,64,256]{2,1,0:T(8,128)(2,1)} %reduce-scatter.8.cloned.1.call-done) | copy-start | bytes 294916
  192.7 5.0 %collective-permute-start = (bf16[1,64,256]{2,1,0:T(8,128)(2,1)S(1)}, bf16[1,64,256]{2,1,0:T(8,128)(2,1)S(1)}, u32[]{:S(2)}, u32[]{:S(2)}) collective-permute-start(bf16[1,64,256]{2,1,0:T(8,128)(2,1)S(1)} %get-tuple-element.205), channel_id=1, source_target_pairs={{0,4},{4,8},{8,12},{1,5},{5,9},{9,13},{2,6},{6,10},{10,14},{3,7},{... | collective-permute-start | bytes 98312 | tf_op jit(solution)/shard_map/ppermute | solution.py:19
  196.1 5.8 %collective-permute-start.1 = (bf16[1,64,256]{2,1,0:T(8,128)(2,1)S(1)}, bf16[1,64,256]{2,1,0:T(8,128)(2,1)S(1)}, u32[]{:S(2)}, u32[]{:S(2)}) collective-permute-start(bf16[1,64,256]{2,1,0:T(8,128)(2,1)S(1)} %get-tuple-element.206), channel_id=1, source_target_pairs={{4,0},{8,4},{12,8},{5,1},{9,5},{13,9},{6,2},{10,6},{14,10},{7,3},{... | collective-permute-start | bytes 98312 | tf_op jit(solution)/shard_map/ppermute | solution.py:21
  201.9 3.8 %collective-permute-start.2 = (bf16[5,1,256]{2,1,0:T(2,128)(2,1)S(1)}, bf16[5,1,256]{2,1,0:T(2,128)(2,1)S(1)}, u32[]{:S(2)}, u32[]{:S(2)}) collective-permute-start(bf16[5,1,256]{2,1,0:T(2,128)(2,1)S(1)} %get-tuple-element.204), channel_id=1, source_target_pairs={{0,2},{1,3},{4,6},{5,7},{8,10},{9,11},{12,14},{13,15},{16,18},{17,... | collective-permute-start | bytes 7688 | tf_op jit(solution)/shard_map/ppermute | solution.py:19
  204.4 5.5 %collective-permute-start.3 = (bf16[5,1,256]{2,1,0:T(2,128)(2,1)S(1)}, bf16[5,1,256]{2,1,0:T(2,128)(2,1)S(1)}, u32[]{:S(2)}, u32[]{:S(2)}) collective-permute-start(bf16[5,1,256]{2,1,0:T(2,128)(2,1)S(1)} %get-tuple-element.203), channel_id=1, source_target_pairs={{2,0},{3,1},{6,4},{7,5},{10,8},{11,9},{14,12},{15,13},{18,16},{19,... | collective-permute-start | bytes 7688 | tf_op jit(solution)/shard_map/ppermute | solution.py:21
Sparse Core Ops, SparseCore 0:
  81.7 14.7 reduce-scatter.9
  163.7 14.6 reduce-scatter.11
  180.7 11.0 reduce-scatter.7
where the time goes:
time: 219 us; the launch traced here: 218 us
  blocking collectives  101 us (46%)
  matrix products  40.5 us (18%)
  waiting for transfers between devices  34.7 us (16%)
  local copies, waits for them, and re-layouts  13.6 us (6%)
  between operations  13.5 us (6%)
  starting transfers between devices  8.52 us (4%)
  other arithmetic  5.96 us (3%)
    all_gather x1, blocking collectives, body(): lax.all_gather(self_key, 'blk', axis=0, tiled=True)  20 us
    all_gather x1, blocking collectives, body(): lax.all_gather(self_value, 'blk', axis=0, tiled=True)  18.1 us
    all_gather x1, blocking collectives, body(): lax.all_gather(cross_value, 'blk', axis=0, tiled=True)  17.3 us
    all_gather x1, blocking collectives, body(): lax.all_gather(cross_key, 'blk', axis=0, tiled=True)  16.3 us
    dot_general x4, matrix products, attend_keys(): jnp.einsum('qhd,khd->hqk', queries.reshape(query_count, head_count, HD),...  15.5 us
    unnamed x5, waiting for transfers between devices  14.8 us
    dot_general x4, matrix products, attend_keys(): jnp.einsum('hqk,khd->qhd', expanded.astype(jnp.bfloat16), values_rows.res...  14 us
    reduce_scatter x1, waiting for transfers between devices, body(): lax.psum_scatter(partial_map.astype(jnp.bfloat16), 'tile', scatter_dimens...  11.2 us
  transfers between devices with their start and end apart: 7, of which 5 were waited for; matrix products, arithmetic and copies ran while one was open for 1% of the time, Pallas kernels for 0%

commit v1 on v0

--- a/solution.py
+++ b/solution.py
@@ -6,6 +6,19 @@
 HD = 64
 CH = 256
 GRID_W = 128
+
+
+def collect(value, axis, dim):
+    ways = lax.axis_size(axis)
+    up = [(d, (d + 1) % ways) for d in range(ways)]
+    down = [(d, (d - 1) % ways) for d in range(ways)]
+    earlier, later = ([value], [value])
+    for _ in range(ways // 2):
+        earlier.append(lax.ppermute(earlier[-1], axis, up))
+    for _ in range((ways - 1) // 2):
+        later.append(lax.ppermute(later[-1], axis, down))
+    line = jnp.concatenate([*earlier[::-1], *later[1:]], axis=dim)
+    return jnp.roll(line, (lax.axis_index(axis) - ways // 2) * value.shape[dim], axis=dim)
 
 
 def padded_2(cells, sides, width):
@@ -111,10 +124,7 @@
     self_value = project_rows(left_normed, self_qkv[2])
     cross_key = project_rows(right_normed, cross_qkv[1])
     cross_value = project_rows(right_normed, cross_qkv[2])
-    pieces = (
-        lax.all_gather(self_key, "blk", axis=0, tiled=True),
-        lax.all_gather(self_value, "blk", axis=0, tiled=True),
-    )
+    pieces = (lax.all_gather(self_key, "blk", axis=0, tiled=True), collect(self_value, "blk", 0))
     self_state = fold_keys(initial_state(self_query), self_query, pieces[0], pieces[1])
     self_mixed = finish_state(self_state)
     self_term = jnp.dot(self_mixed, self_out, preferred_element_type=jnp.float32)

time: 219 us -> 212 us (0.968)
  blocking collectives: 101 us -> 81.9 us
  waiting for transfers between devices: 34.7 us -> 40.7 us
  starting transfers between devices: 8.52 us -> 13.4 us
    all_gather x1 -> x0, blocking collectives: 18.1 us -> none  [body(): lax.all_gather(self_value, 'blk', axis=0, tiled=True)]
    ppermute x0 -> x3, starting transfers between devices: none -> 4.93 us  [the longest x2 2.83 us: collect(): earlier.append(lax.ppermute(earlier[-1], axis, up))]
    ppermute x0 -> x3, waiting for transfers between devices: none -> 4.81 us  [the longest x2 4.81 us: collect(): earlier.append(lax.ppermute(earlier[-1], axis, up))]
    all_gather x1, blocking collectives: 9.72 us -> 7.38 us  [body(): lax.all_gather(right_tokens, 'tile', axis=2, tiled=True)]
    unnamed x27 -> x44, local copies, waits for them, and re-layouts: 6.94 us -> 7.05 us
  transfers between devices with their start and end apart: 7 -> 10, of which waited for: 5 -> 6; matrix products, arithmetic and copies ran while one was open for 1% -> 3% of each run, Pallas kernels for 0% -> 0%
where the time goes in v1:
time: 212 us; the launch traced here: 211 us
  blocking collectives  81.9 us (39%)
  waiting for transfers between devices  40.7 us (19%)
  matrix products  40.5 us (19%)
  local copies, waits for them, and re-layouts  14 us (7%)
  between operations  13.6 us (6%)
  starting transfers between devices  13.4 us (6%)
  other arithmetic  6.53 us (3%)
    all_gather x1, blocking collectives, body(): lax.all_gather(self_key, 'blk', axis=0, tiled=True)  21.9 us
    all_gather x1, blocking collectives, body(): lax.all_gather(cross_value, 'blk', axis=0, tiled=True)  17.7 us
    all_gather x1, blocking collectives, body(): lax.all_gather(cross_key, 'blk', axis=0, tiled=True)  16.3 us
    unnamed x5, waiting for transfers between devices  16 us
    dot_general x4, matrix products, attend_keys(): jnp.einsum('qhd,khd->hqk', queries.reshape(query_count, head_count, HD),...  15.5 us
    dot_general x4, matrix products, attend_keys(): jnp.einsum('hqk,khd->qhd', expanded.astype(jnp.bfloat16), values_rows.res...  14 us
    reduce_scatter x1, waiting for transfers between devices, body(): lax.psum_scatter(partial_map.astype(jnp.bfloat16), 'tile', scatter_dimens...  11.2 us
    all_gather x1, blocking collectives, body(): lax.all_gather(left_tokens, 'tile', axis=2, tiled=True)  11 us
  transfers between devices with their start and end apart: 10, of which 6 were waited for; matrix products, arithmetic and copies ran while one was open for 3% of the time, Pallas kernels for 0%

profile of v1, /device:TPU:0, one launch (start us, length us, event | category | flops | bytes accessed | tf_op | source)
XLA Modules:
  0.0 210.8 jit_solution(2752539351493203461)
XLA Ops:
  6.5 11.0 %all_gather.18 = bf16[1,384,768]{2,1,0:T(8,128)(2,1)S(1)} all-gather(bf16[1,384,384]{2,1,0:T(8,128)(2,1)} %param.12), channel_id=1, replica_groups=mesh['groups'=2,'blk'=4,'tile'=2,'pair'=2] {'tile'}, dimensions={2}, use_global_device_ids=true | all-gather | bytes 884736 | tf_op jit(solution)/shard_map/all_gather | solution.py:116
  18.1 1.4 convolution_convert_fusion.6
  19.5 1.8 collective-permute-start
  21.3 2.1 collective-permute-start.2
  24.2 21.9 %all_gather.19 = bf16[1536,256]{1,0:T(8,128)(2,1)} all-gather(bf16[384,256]{1,0:T(8,128)(2,1)S(1)} %convolution_convert_fusion.8), channel_id=1, replica_groups=mesh['groups'=2,'blk'=4,'tile'=2,'pair'=2] {'blk'}, dimensions={0}, use_global_device_ids=true | all-gather | bytes 983040 | tf_op jit(solution)/shard_map/all_gather | solution.py:127
  46.1 7.4 %all_gather.20 = bf16[1,384,768]{2,1,0:T(8,128)(2,1)S(1)} all-gather(bf16[1,384,384]{2,1,0:T(8,128)(2,1)S(1)} %copy-done.9), channel_id=1, replica_groups=mesh['groups'=2,'blk'=4,'tile'=2,'pair'=2] {'tile'}, dimensions={2}, use_global_device_ids=true | all-gather | bytes 884736 | tf_op jit(solution)/shard_map/all_gather | solution.py:117
  53.6 1.0 collective-permute-start.1
  54.7 0.8 copy.27
  55.5 0.9 fusion.45
  56.3 4.8 %collective-permute-done.1 = bf16[384,256]{1,0:T(8,128)(2,1)S(1)} collective-permute-done((bf16[384,256]{1,0:T(8,128)(2,1)S(1)}, bf16[384,256]{1,0:T(8,128)(2,1)S(1)}, u32[]{:S(2)}, u32[]{:S(2)}) %collective-permute-start.1) | collective-permute-done | bytes 196640 | tf_op jit(solution)/shard_map/ppermute | solution.py:17
  61.6 19.8 %while.30 = (s32[]{:T(128)}, f32[4,384]{1,0:T(4,128)S(1)}, f32[4,384]{1,0:T(4,128)S(1)}, f32[384,256]{0,1:T(8,128)S(1)}, bf16[2,768,256]{2,1,0:T(8,128)(2,1)}, /...) while((s32[]{:T(128)}, f32[4,384]{1,0:T(4,128)S(1)}, ...), condition=%wide.region_5.6_spmd.clone, body=%wide.region_2.5_spmd.clone.sunk | while | flops 311632896 | bytes 38043784 | solution.py:100
  61.6 1.1 constant_dynamic-slice_fusion.7
  62.9 3.9 %bitcast_reduce_fusion.4 = (f32[4,384]{1,0:T(4,128)S(1)}, f32[4,768,384]{2,1,0:T(8,128)}) fusion(bf16[768,4,64]{0,2,1:T(8,128)(2,1)S(1)} %bitcast.186, bf16[384,4,64]{0,2,1:T(8,128)(2,1)} %bitcast.198), kind=kOutput, calls=%fused_computation.1.clone.1 | convolution fusion | flops 153352704 | bytes 5314560 | tf_op jit(solution)/shard_map/while/body/eval_jaxpr/qhd,khd->hqk/dot_general | solution.py:67
  66.9 3.5 %fusion.112 = f32[384,4,64]{0,2,1:T(8,128)S(1)} fusion(bf16[768,4,64]{0,2,1:T(8,128)(2,1)S(1)} %bitcast.187, f32[4,768,384]{2,1,0:T(8,128)} %get-tuple-element.315, f32[4,384]{1,0:T(4,128)S(1)} %get-tuple-element.350, f32[384,4,64]{0,2,1:T(8,128)S(1)} %bitcast.192, f32[384,4]{0,1:T(4,128)S(1)} %get-tuple-element.317), kind=kOutput, calls=%fused_computation.9.clone.1 | convolution fusion | flops 154730496 | bytes 5910528 | tf_op jit(solution)/shard_map/while/body/eval_jaxpr/hqk,khd->qhd/dot_general | solution.py:77
  71.5 1.1 constant_dynamic-slice_fusion.7
  72.7 3.9 %bitcast_reduce_fusion.4 = (f32[4,384]{1,0:T(4,128)S(1)}, f32[4,768,384]{2,1,0:T(8,128)}) fusion(bf16[768,4,64]{0,2,1:T(8,128)(2,1)S(1)} %bitcast.186, bf16[384,4,64]{0,2,1:T(8,128)(2,1)} %bitcast.198), kind=kOutput, calls=%fused_computation.1.clone.1 | convolution fusion | flops 153352704 | bytes 5314560 | tf_op jit(solution)/shard_map/while/body/eval_jaxpr/qhd,khd->hqk/dot_general | solution.py:67
  76.8 3.5 %fusion.112 = f32[384,4,64]{0,2,1:T(8,128)S(1)} fusion(bf16[768,4,64]{0,2,1:T(8,128)(2,1)S(1)} %bitcast.187, f32[4,768,384]{2,1,0:T(8,128)} %get-tuple-element.315, f32[4,384]{1,0:T(4,128)S(1)} %get-tuple-element.350, f32[384,4,64]{0,2,1:T(8,128)S(1)} %bitcast.192, f32[384,4]{0,1:T(4,128)S(1)} %get-tuple-element.317), kind=kOutput, calls=%fused_computation.9.clone.1 | convolution fusion | flops 154730496 | bytes 5910528 | tf_op jit(solution)/shard_map/while/body/eval_jaxpr/hqk,khd->qhd/dot_general | solution.py:77
  81.4 1.4 convolution_convert_fusion.1
  82.8 1.1 copy.34
  84.0 1.4 convolution_convert_fusion.3
  85.4 1.4 convolution_convert_fusion.5
  86.8 17.7 %all_gather.23 = bf16[1536,256]{1,0:T(8,128)(2,1)S(1)} all-gather(bf16[384,256]{1,0:T(8,128)(2,1)S(1)} %convolution_convert_fusion.3), channel_id=1, replica_groups=mesh['groups'=2,'blk'=4,'tile'=2,'pair'=2] {'blk'}, dimensions={0}, use_global_device_ids=true | all-gather | bytes 983040 | tf_op jit(solution)/shard_map/all_gather | solution.py:140
  104.5 16.3 %all_gather.21 = bf16[1536,256]{1,0:T(8,128)(2,1)} all-gather(bf16[384,256]{1,0:T(8,128)(2,1)S(1)} %convolution_convert_fusion.5), channel_id=1, replica_groups=mesh['groups'=2,'blk'=4,'tile'=2,'pair'=2] {'blk'}, dimensions={0}, use_global_device_ids=true | all-gather | bytes 983040 | tf_op jit(solution)/shard_map/all_gather | solution.py:139
  120.8 1.2 copy.35
  122.8 7.6 %all_gather.22 = bf16[384,768]{1,0:T(8,128)(2,1)S(1)} all-gather(bf16[384,384]{1,0:T(8,128)(2,1)S(1)} %fusion.51), channel_id=1, replica_groups=mesh['groups'=2,'blk'=4,'tile'=2,'pair'=2] {'tile'}, dimensions={1}, use_global_device_ids=true | all-gather | bytes 884736 | tf_op jit(solution)/shard_map/all_gather | solution.py:135
  130.9 1.4 convolution_convert_fusion.4
  132.2 0.8 copy.30
  133.1 19.8 %while.31 = (s32[]{:T(128)}, f32[4,384]{1,0:T(4,128)S(1)}, f32[4,384]{1,0:T(4,128)S(1)}, f32[384,256]{0,1:T(8,128)S(1)}, bf16[2,768,256]{2,1,0:T(8,128)(2,1)}, /...) while((s32[]{:T(128)}, f32[4,384]{1,0:T(4,128)S(1)}, ...), condition=%wide.region_14.15_spmd.clone, body=%wide.region_11.14_spmd.clone.sunk | while | flops 311632896 | bytes 38043784 | solution.py:100
  133.1 1.1 constant_dynamic-slice_fusion.8
  134.3 3.9 %bitcast_reduce_fusion.5 = (f32[4,384]{1,0:T(4,128)S(1)}, f32[4,768,384]{2,1,0:T(8,128)}) fusion(bf16[768,4,64]{0,2,1:T(8,128)(2,1)S(1)} %bitcast.188, bf16[384,4,64]{0,2,1:T(8,128)(2,1)} %bitcast.199), kind=kOutput, calls=%fused_computation.19.clone.1 | convolution fusion | flops 153352704 | bytes 5314560 | tf_op jit(solution)/shard_map/while/body/eval_jaxpr/qhd,khd->hqk/dot_general | solution.py:67
  138.4 3.5 %fusion.120 = f32[384,4,64]{0,2,1:T(8,128)S(1)} fusion(bf16[768,4,64]{0,2,1:T(8,128)(2,1)S(1)} %bitcast.189, f32[4,768,384]{2,1,0:T(8,128)} %get-tuple-element.328, f32[4,384]{1,0:T(4,128)S(1)} %get-tuple-element.377, f32[384,4,64]{0,2,1:T(8,128)S(1)} %bitcast.190, f32[384,4]{0,1:T(4,128)S(1)} %get-tuple-element.330), kind=kOutput, calls=%fused_computation.27.clone.1 | convolution fusion | flops 154730496 | bytes 5910528 | tf_op jit(solution)/shard_map/while/body/eval_jaxpr/hqk,khd->qhd/dot_general | solution.py:77
  143.0 1.1 constant_dynamic-slice_fusion.8
  144.2 3.9 %bitcast_reduce_fusion.5 = (f32[4,384]{1,0:T(4,128)S(1)}, f32[4,768,384]{2,1,0:T(8,128)}) fusion(bf16[768,4,64]{0,2,1:T(8,128)(2,1)S(1)} %bitcast.188, bf16[384,4,64]{0,2,1:T(8,128)(2,1)} %bitcast.199), kind=kOutput, calls=%fused_computation.19.clone.1 | convolution fusion | flops 153352704 | bytes 5314560 | tf_op jit(solution)/shard_map/while/body/eval_jaxpr/qhd,khd->hqk/dot_general | solution.py:67
  148.3 3.5 %fusion.120 = f32[384,4,64]{0,2,1:T(8,128)S(1)} fusion(bf16[768,4,64]{0,2,1:T(8,128)(2,1)S(1)} %bitcast.189, f32[4,768,384]{2,1,0:T(8,128)} %get-tuple-element.328, f32[4,384]{1,0:T(4,128)S(1)} %get-tuple-element.377, f32[384,4,64]{0,2,1:T(8,128)S(1)} %bitcast.190, f32[384,4]{0,1:T(4,128)S(1)} %get-tuple-element.330), kind=kOutput, calls=%fused_computation.27.clone.1 | convolution fusion | flops 154730496 | bytes 5910528 | tf_op jit(solution)/shard_map/while/body/eval_jaxpr/hqk,khd->qhd/dot_general | solution.py:77
  152.9 1.4 convolution_convert_fusion
  154.3 1.1 copy.36
  155.5 16.0 %reduce-scatter.12.cloned.1.call-done = bf16[384,384]{1,0:T(8,128)(2,1)} async-done(((bf16[768,384]{1,0:T(8,128)(2,1)}), bf16[384,384]{1,0:T(8,128)(2,1)}) %reduce-scatter.12.cloned.1.call-update) | async-done | bytes 294928
  171.4 1.2 copy.37
  172.6 0.9 convolution_convert_fusion.2
  173.6 11.2 %reduce-scatter.8.cloned.1.call-done = bf16[3,64,256]{2,1,0:T(8,128)(2,1)} async-done(((bf16[3,128,256]{2,1,0:T(8,128)(2,1)}), bf16[3,64,256]{2,1,0:T(8,128)(2,1)}) %reduce-scatter.8.cloned.1.call-update) | async-done | bytes 98320 | tf_op jit(solution)/shard_map/reduce_scatter | solution.py:155
  184.8 1.0 broadcast_maximum_fusion
  185.8 3.4 %collective-permute-start.3 = (bf16[1,64,256]{2,1,0:T(8,128)(2,1)S(1)}, bf16[1,64,256]{2,1,0:T(8,128)(2,1)S(1)}, u32[]{:S(2)}, u32[]{:S(2)}) collective-permute-start(bf16[1,64,256]{2,1,0:T(8,128)(2,1)S(1)} %get-tuple-element.219), channel_id=1, source_target_pairs={{0,4},{4,8},{8,12},{1,5},{5,9},{9,13},{2,6},{6,10},{10,14},{3,7},{... | collective-permute-start | bytes 98312 | tf_op jit(solution)/shard_map/ppermute | solution.py:32
  189.1 1.3 collective-permute-start.4
  190.7 4.2 %collective-permute-done.4 = bf16[1,64,256]{2,1,0:T(8,128)(2,1)S(1)} collective-permute-done((bf16[1,64,256]{2,1,0:T(8,128)(2,1)S(1)}, bf16[1,64,256]{2,1,0:T(8,128)(2,1)S(1)}, u32[]{:S(2)}, u32[]{:S(2)}) %collective-permute-start.4) | collective-permute-done | bytes 32800 | tf_op jit(solution)/shard_map/ppermute | solution.py:34
  195.0 2.5 %collective-permute-start.5 = (bf16[5,1,256]{2,1,0:T(2,128)(2,1)S(1)}, bf16[5,1,256]{2,1,0:T(2,128)(2,1)S(1)}, u32[]{:S(2)}, u32[]{:S(2)}) collective-permute-start(bf16[5,1,256]{2,1,0:T(2,128)(2,1)S(1)} %get-tuple-element.218), channel_id=1, source_target_pairs={{0,2},{1,3},{4,6},{5,7},{8,10},{9,11},{12,14},{13,15},{16,18},{17,... | collective-permute-start | bytes 7688 | tf_op jit(solution)/shard_map/ppermute | solution.py:32
  197.4 1.3 collective-permute-start.6
  198.8 4.2 %collective-permute-done.6 = bf16[5,1,256]{2,1,0:T(2,128)(2,1)S(1)} collective-permute-done((bf16[5,1,256]{2,1,0:T(2,128)(2,1)S(1)}, bf16[5,1,256]{2,1,0:T(2,128)(2,1)S(1)}, u32[]{:S(2)}, u32[]{:S(2)}) %collective-permute-start.6) | collective-permute-done | bytes 2592 | tf_op jit(solution)/shard_map/ppermute | solution.py:34
  203.3 1.1 fusion.47
  (112 shorter events, 9.5 us)
Async XLA Ops:
  6.5 196.7 %copy-start = (bf16[3,3,256,256]{3,2,1,0:T(8,128)(2,1)S(1)}, bf16[3,3,256,256]{3,2,1,0:T(8,128)(2,1)}, u32[]{:S(2)}) copy-start(bf16[3,3,256,256]{3,2,1,0:T(8,128)(2,1)} %param.19) | copy-start | bytes 3538948
  6.5 114.3 %reduce-scatter.10.cloned.1.call-start = ((), (), s32[]{:S(2)}) async-start(), calls=%async_computation.4 | async-start | bytes 884736
  17.7 5.7 %copy-start.14 = (bf16[3,768,256]{2,1,0:T(8,128)(2,1)S(1)}, bf16[3,768,256]{2,1,0:T(8,128)(2,1)}, u32[]{:S(2)}) copy-start(bf16[3,768,256]{2,1,0:T(8,128)(2,1)} %param.14) | copy-start | bytes 3538948
  19.5 34.2 %collective-permute-start = (bf16[384,256]{1,0:T(8,128)(2,1)S(1)}, bf16[384,256]{1,0:T(8,128)(2,1)S(1)}, u32[]{:S(2)}, u32[]{:S(2)}) collective-permute-start(bf16[384,256]{1,0:T(8,128)(2,1)S(1)} %convolution_convert_fusion.6), channel_id=1, source_target_pairs={{0,4},{4,8},{8,12},{12,0},{1,5},{5,9},{9,13},{13,1},{2,6},{6,10},{... | collective-permute-start | bytes 589832 | tf_op jit(solution)/shard_map/ppermute | solution.py:17
  21.3 39.9 %collective-permute-start.2 = (bf16[384,256]{1,0:T(8,128)(2,1)S(1)}, bf16[384,256]{1,0:T(8,128)(2,1)S(1)}, u32[]{:S(2)}, u32[]{:S(2)}) collective-permute-start(bf16[384,256]{1,0:T(8,128)(2,1)S(1)} %convolution_convert_fusion.6), channel_id=1, source_target_pairs={{0,12},{4,0},{8,4},{12,8},{1,13},{5,1},{9,5},{13,9},{2,14},{6,2},{... | collective-permute-start | bytes 589832 | tf_op jit(solution)/shard_map/ppermute | solution.py:19
  23.8 22.3 %copy-start.9 = (bf16[1,384,384]{2,1,0:T(8,128)(2,1)S(1)}, bf16[1,384,384]{2,1,0:T(8,128)(2,1)}, u32[]{:S(2)}) copy-start(bf16[1,384,384]{2,1,0:T(8,128)(2,1)} %param.13) | copy-start | bytes 884740
  53.5 7.7 %copy-start.3 = (bf16[1,384,768]{2,1,0:T(8,128)(2,1)}, bf16[1,384,768]{2,1,0:T(8,128)(2,1)S(1)}, u32[]{:S(2)}) copy-start(bf16[1,384,768]{2,1,0:T(8,128)(2,1)S(1)} %all_gather.20) | copy-start | bytes 1769476
  53.6 7.5 %collective-permute-start.1 = (bf16[384,256]{1,0:T(8,128)(2,1)S(1)}, bf16[384,256]{1,0:T(8,128)(2,1)S(1)}, u32[]{:S(2)}, u32[]{:S(2)}) collective-permute-start(bf16[384,256]{1,0:T(8,128)(2,1)S(1)} %collective-permute-done), channel_id=1, source_target_pairs={{0,4},{4,8},{8,12},{12,0},{1,5},{5,9},{9,13},{13,1},{2,6},{6,10},{... | collective-permute-start | bytes 589832 | tf_op jit(solution)/shard_map/ppermute | solution.py:17
  54.6 6.6 %copy-start.11 = (f32[384]{0:T(512)}, f32[384]{0:T(512)S(1)}, u32[]{:S(2)}) copy-start(f32[384]{0:T(512)S(1)} %broadcast_multiply_fusion.1) | copy-start | bytes 4612
  66.9 3.8 %copy-start.1 = (f32[4,768,384]{2,1,0:T(8,128)S(1)}, f32[4,768,384]{2,1,0:T(8,128)}, u32[]{:S(2)}) copy-start(f32[4,768,384]{2,1,0:T(8,128)} %get-tuple-element.315) | copy-start | bytes 14155780 | tf_op jit(solution)/shard_map/while
  76.8 3.8 %copy-start.1 = (f32[4,768,384]{2,1,0:T(8,128)S(1)}, f32[4,768,384]{2,1,0:T(8,128)}, u32[]{:S(2)}) copy-start(f32[4,768,384]{2,1,0:T(8,128)} %get-tuple-element.315) | copy-start | bytes 14155780 | tf_op jit(solution)/shard_map/while
  82.8 1.2 copy-start.13
  82.8 1.2 copy-start.4
  82.8 1.2 copy-start.12
  83.9 87.5 %reduce-scatter.12.cloned.1.call-start = ((), (), s32[]{:S(2)}) async-start(), calls=%async_computation.5 | async-start | bytes 884736
  86.8 35.2 %copy-start.7 = (bf16[1,384,384]{2,1,0:T(8,128)(2,1)S(1)}, bf16[1,384,384]{2,1,0:T(8,128)(2,1)}, u32[]{:S(2)}) copy-start(bf16[1,384,384]{2,1,0:T(8,128)(2,1)} %param.12) | copy-start | bytes 884740
  122.1 0.7 copy-start.5
  138.4 3.8 %copy-start.2 = (f32[4,768,384]{2,1,0:T(8,128)S(1)}, f32[4,768,384]{2,1,0:T(8,128)}, u32[]{:S(2)}) copy-start(f32[4,768,384]{2,1,0:T(8,128)} %get-tuple-element.328) | copy-start | bytes 14155780 | tf_op jit(solution)/shard_map/while
  148.3 3.8 %copy-start.2 = (f32[4,768,384]{2,1,0:T(8,128)S(1)}, f32[4,768,384]{2,1,0:T(8,128)}, u32[]{:S(2)}) copy-start(f32[4,768,384]{2,1,0:T(8,128)} %get-tuple-element.328) | copy-start | bytes 14155780 | tf_op jit(solution)/shard_map/while
  154.3 18.3 %copy-start.6 = (bf16[384,384]{1,0:T(8,128)(2,1)S(1)}, bf16[384,384]{1,0:T(8,128)(2,1)}, u32[]{:S(2)}) copy-start(bf16[384,384]{1,0:T(8,128)(2,1)} %copy-done.5) | copy-start | bytes 884740
  154.3 18.3 %copy-start.10 = (bf16[384,256]{1,0:T(8,128)(2,1)S(1)}, bf16[384,256]{1,0:T(8,128)(2,1)}, u32[]{:S(2)}) copy-start(bf16[384,256]{1,0:T(8,128)(2,1)} %param.18) | copy-start | bytes 589828
  155.4 29.4 %reduce-scatter.8.cloned.1.call-start = ((), (), s32[]{:S(2)}) async-start(), calls=%async_computation.3 | async-start | bytes 294912 | tf_op jit(solution)/shard_map/reduce_scatter | solution.py:155
  184.8 18.3 %copy-start.8 = (bf16[3,64,256]{2,1,0:T(8,128)(2,1)S(1)}, bf16[3,64,256]{2,1,0:T(8,128)(2,1)}, u32[]{:S(2)}) copy-start(bf16[3,64,256]{2,1,0:T(8,128)(2,1)} %reduce-scatter.8.cloned.1.call-done) | copy-start | bytes 294916
  185.8 5.0 %collective-permute-start.3 = (bf16[1,64,256]{2,1,0:T(8,128)(2,1)S(1)}, bf16[1,64,256]{2,1,0:T(8,128)(2,1)S(1)}, u32[]{:S(2)}, u32[]{:S(2)}) collective-permute-start(bf16[1,64,256]{2,1,0:T(8,128)(2,1)S(1)} %get-tuple-element.219), channel_id=1, source_target_pairs={{0,4},{4,8},{8,12},{1,5},{5,9},{9,13},{2,6},{6,10},{10,14},{3,7},{... | collective-permute-start | bytes 98312 | tf_op jit(solution)/shard_map/ppermute | solution.py:32
  189.1 5.8 %collective-permute-start.4 = (bf16[1,64,256]{2,1,0:T(8,128)(2,1)S(1)}, bf16[1,64,256]{2,1,0:T(8,128)(2,1)S(1)}, u32[]{:S(2)}, u32[]{:S(2)}) collective-permute-start(bf16[1,64,256]{2,1,0:T(8,128)(2,1)S(1)} %get-tuple-element.220), channel_id=1, source_target_pairs={{4,0},{8,4},{12,8},{5,1},{9,5},{13,9},{6,2},{10,6},{14,10},{7,3},{... | collective-permute-start | bytes 98312 | tf_op jit(solution)/shard_map/ppermute | solution.py:34
  195.0 3.8 %collective-permute-start.5 = (bf16[5,1,256]{2,1,0:T(2,128)(2,1)S(1)}, bf16[5,1,256]{2,1,0:T(2,128)(2,1)S(1)}, u32[]{:S(2)}, u32[]{:S(2)}) collective-permute-start(bf16[5,1,256]{2,1,0:T(2,128)(2,1)S(1)} %get-tuple-element.218), channel_id=1, source_target_pairs={{0,2},{1,3},{4,6},{5,7},{8,10},{9,11},{12,14},{13,15},{16,18},{17,... | collective-permute-start | bytes 7688 | tf_op jit(solution)/shard_map/ppermute | solution.py:32
  197.4 5.5 %collective-permute-start.6 = (bf16[5,1,256]{2,1,0:T(2,128)(2,1)S(1)}, bf16[5,1,256]{2,1,0:T(2,128)(2,1)S(1)}, u32[]{:S(2)}, u32[]{:S(2)}) collective-permute-start(bf16[5,1,256]{2,1,0:T(2,128)(2,1)S(1)} %get-tuple-element.217), channel_id=1, source_target_pairs={{2,0},{3,1},{6,4},{7,5},{10,8},{11,9},{14,12},{15,13},{18,16},{19,... | collective-permute-start | bytes 7688 | tf_op jit(solution)/shard_map/ppermute | solution.py:34
Sparse Core Ops, SparseCore 0:
  84.0 14.1 reduce-scatter.9
  155.5 15.8 reduce-scatter.11
  173.7 11.0 reduce-scatter.7
